TPU v7x, 256 devices: a whole 4x4x8 slice. The times are simulated.
256 devices in a mesh: src: 8 (over x, y_hi), tgt: 32 (over z, y_lo, core).
Axes of the slice: x: 4, y: 4 (y_hi: 2, y_lo: 2; y = y_hi * 2 + y_lo), z: 8, core: 2. Of those that a mesh axis runs over, the one named last changes fastest.
Arguments:
- source_feats: bfloat16 [1, 32, 32, 1024], P(None, 'src', None, 'tgt'), may hold values from -200 to 200
- target_feats: bfloat16 [1, 128, 32, 1024], P(None, 'tgt', None, 'src'), may hold values from -200 to 200
- conv_one: bfloat16 [3, 3, 3, 3, 1, 16], replicated, may hold values from -1 to 1
- bias_one: float32 [16], replicated, may hold values from -1.5 to 1.5
- conv_two: bfloat16 [3, 3, 3, 3, 16, 16], replicated, may hold values from -0.25 to 0.25
- bias_two: float32 [16], replicated, may hold values from -1.5 to 1.5
- conv_three: bfloat16 [3, 3, 3, 3, 16, 1], replicated, may hold values from -0.25 to 0.25
- bias_three: float32 [1], replicated, may hold values from -1.5 to 1.5
Outputs:
- scores: bfloat16 [1, 32, 128, 32, 32], P(None, 'src', 'tgt')
All inputs are finite; a program needn't handle non-finite values.
Results may differ from a plain program's by a relative error of at most 0.0049.
The roundings to bfloat16 on the way count: a program that leaves them out, or rounds other values in their place, can miss the bound.
Values may be sent and summed in bfloat16 or wider, within the bound.
A program may use at most 256 MiB of HBM per device.

v0:
```python
import functools

import jax
import jax.numpy as jnp
from jax import lax
from jax.experimental import pallas as pl
from jax.experimental.pallas import tpu as pltpu
from jax.sharding import PartitionSpec as P

F32, BF = jnp.float32, jnp.bfloat16

MESH = pl.DeviceIdType.MESH
EPS = 1e-6
SIDES = [(ds, dt) for ds in (-1, 0, 1) for dt in (-1, 0, 1) if ds or dt]


def halo_span(d):
    if d == 0:
        return 0, 4, 3
    return (1, 3, 0) if d > 0 else (0, 3, 7)


def volume_kernel(ns, nt, src_ref, tgt_ref, vol, gs, gt, own, s_send, s_recv, t_send, t_recv, h_send, h_recv):
    s, t = lax.axis_index("src"), lax.axis_index("tgt")
    ch_s, ch_t = src_ref.shape[-1], tgt_ref.shape[-1]

    vol[...] = jnp.zeros_like(vol)
    barrier = pltpu.get_barrier_semaphore()

    def greet(ds, dt):
        pl.semaphore_signal(barrier, inc=1, device_id=(s + ds, t + dt), device_id_type=MESH)

    @pl.loop(1, nt)
    def _(r):
        pl.semaphore_signal(barrier, inc=1, device_id=(s, lax.rem(t + r, nt)), device_id_type=MESH)

    @pl.loop(1, ns)
    def _(r):
        pl.semaphore_signal(barrier, inc=1, device_id=(lax.rem(s + r, ns), t), device_id_type=MESH)

    def there(ds, dt):
        return (s + ds >= 0) & (s + ds < ns) & (t + dt >= 0) & (t + dt < nt)

    count = ns - 1 + nt - 1
    for ds, dt in SIDES:
        if ds and dt:
            count = count + jnp.where(there(ds, dt), 1, 0)

            @pl.when(there(ds, dt))
            def _():
                greet(ds, dt)

    eye = (lax.broadcasted_iota(jnp.int32, (ch_s, ch_s), 0)
           == lax.broadcasted_iota(jnp.int32, (ch_s, ch_s), 1)).astype(BF)
    gs[t] = lax.dot_general(eye, src_ref[...], (((1,), (1,)), ((), ())),
                            preferred_element_type=F32).astype(BF)
    gt[s] = tgt_ref[...]
    pl.semaphore_wait(barrier, count)

    def send_s(r):
        return pltpu.make_async_remote_copy(
            src_ref=gs.at[t], dst_ref=gs.at[t], send_sem=s_send.at[r - 1], recv_sem=s_recv.at[r - 1],
            device_id=(s, lax.rem(t + r, nt)), device_id_type=MESH)

    def got_s(r):
        at = gs.at[lax.rem(t + nt - r, nt)]
        return pltpu.make_async_remote_copy(
            src_ref=at, dst_ref=at, send_sem=s_send.at[r - 1], recv_sem=s_recv.at[r - 1],
            device_id=(s, lax.rem(t + r, nt)), device_id_type=MESH)

    def send_t(r):
        return pltpu.make_async_remote_copy(
            src_ref=tgt_ref, dst_ref=gt.at[s], send_sem=t_send.at[r - 1], recv_sem=t_recv.at[r - 1],
            device_id=(lax.rem(s + r, ns), t), device_id_type=MESH)

    def got_t(r):
        at = gt.at[lax.rem(s + ns - r, ns)]
        return pltpu.make_async_remote_copy(
            src_ref=at, dst_ref=at, send_sem=t_send.at[r - 1], recv_sem=t_recv.at[r - 1],
            device_id=(lax.rem(s + r, ns), t), device_id_type=MESH)

    @pl.loop(1, ns)
    def _(r):
        send_t(r).start()

    @pl.loop(1, nt)
    def _(r):
        send_s(r).start()

    @pl.loop(1, nt)
    def _(r):
        got_s(r).wait_recv()

    sq = None
    for c in range(nt):
        x = gs[c].astype(F32)
        x = x * x
        for q in range(ch_s // 8):
            p = x[8 * q:8 * q + 8]
            sq = p if sq is None else sq + p
    inv_s = lax.rsqrt(jnp.sum(sq, axis=0, keepdims=True) + EPS)

    @pl.loop(1, ns)
    def _(r):
        got_t(r).wait_recv()

    sq = None
    for c in range(ns):
        x = gt[c].astype(F32)
        x = x * x
        sq = x if sq is None else sq + x
    inv_t = lax.rsqrt(jnp.sum(sq, axis=1, keepdims=True) + EPS)

    per = ch_t // ch_s
    acc = jnp.zeros((128, 128), F32)
    for c in range(ns):
        left = jnp.concatenate([gs[c * per + q] for q in range(per)], 0)
        left = (left.astype(F32) * inv_s).astype(BF)
        right = (gt[c].astype(F32) * inv_t).astype(BF)
        acc = acc + jnp.dot(right, left, preferred_element_type=F32)
    v = acc.T
    block = lax.broadcasted_iota(jnp.int32, (8, 128), 1) // 32
    for i in range(4):
        for k in range(4):
            u = None
            for hi in range(4):
                w = v[32 * i + 8 * hi:32 * i + 8 * hi + 8]
                w = pltpu.roll(w, (32 * (hi - k)) % 128, 1) if hi != k else w
                u = w if u is None else jnp.where(block == hi, w, u)
            u = u.astype(BF)
            own[i, k] = u
            vol[3 + i, 3 + k] = u

    def halo(n, ds, dt):
        i0, ni, i1 = halo_span(ds)
        k0, nk, k1 = halo_span(dt)
        return pltpu.make_async_remote_copy(
            src_ref=own.at[pl.ds(i0, ni), pl.ds(k0, nk)], dst_ref=vol.at[pl.ds(i1, ni), pl.ds(k1, nk)],
            send_sem=h_send.at[n], recv_sem=h_recv.at[n], device_id=(s + ds, t + dt), device_id_type=MESH)

    for n, (ds, dt) in enumerate(SIDES):
        @pl.when(there(ds, dt))
        def _():
            halo(n, ds, dt).start()

    for n, (ds, dt) in enumerate(SIDES):
        @pl.when(there(-ds, -dt))
        def _():
            halo(n, ds, dt).wait_recv()

    for n, (ds, dt) in enumerate(SIDES):
        @pl.when(there(ds, dt))
        def _():
            halo(n, ds, dt).wait_send()

    @pl.loop(1, nt)
    def _(r):
        send_s(r).wait_send()

    @pl.loop(1, ns)
    def _(r):
        send_t(r).wait_send()


def volume_call(ns, nt, src, tgt):
    vm = pl.BlockSpec(memory_space=pltpu.VMEM)
    dma = pltpu.SemaphoreType.DMA
    return pl.pallas_call(
        functools.partial(volume_kernel, ns, nt),
        out_shape=jax.ShapeDtypeStruct((10, 10, 8, 128), BF),
        in_specs=[vm, vm], out_specs=vm,
        scratch_shapes=[
            pltpu.VMEM((nt, src.shape[-1], 128), BF),
            pltpu.VMEM((ns, 128, tgt.shape[-1]), BF),
            pltpu.VMEM((4, 4, 8, 128), BF),
            dma((nt - 1,)), dma((nt - 1,)), dma((ns - 1,)), dma((ns - 1,)), dma((8,)), dma((8,)),
        ],
        compiler_params=pltpu.CompilerParams(collective_id=0, has_side_effects=True, vmem_limit_bytes=40 << 20),
    )(src, tgt)


def conv_weights(conv_one, conv_two, conv_three):
    j = jnp.arange(8)[:, None]
    at = jnp.array([0, 1, 2, 3, 4, 5, 6, 7, 8, 90, 90, 90, 90, 90, 90, -1])[None, :]
    hot1 = jnp.stack([(at - j + 1 == b) for b in range(3)]).astype(BF)
    w1 = jnp.einsum("bjJ,abegd->jdaegJ", hot1, conv_one[:, :, :, :, 0, :]).reshape(128, 432)
    w2 = jnp.transpose(conv_two, (3, 5, 0, 2, 1, 4)).reshape(48, 432)
    at3 = (jnp.arange(10) - 1)[None, :]
    hot3 = jnp.stack([(at3 - j + 1 == b) for b in range(3)]).astype(BF)
    w3 = jnp.einsum("bjJ,abegc->gjaeJc", hot3, conv_three[..., 0]).reshape(24, 1440)
    return w1, w2, w3


def rolled(x, by):
    return pltpu.roll(x, by % 128, 1)


def conv_kernel(ns, nt, u_ref, w1_ref, b1_ref, w2_ref, b2_ref, w3_ref, b3_ref, o_ref, z, act1, act2):
    s, t = lax.axis_index("src"), lax.axis_index("tgt")
    lane = lax.broadcasted_iota(jnp.int32, (8, 128), 1)
    row = lax.broadcasted_iota(jnp.int32, (8, 128), 0)
    lane16 = lax.broadcasted_iota(jnp.int32, (16, 128), 1)
    first8, last8 = lane % 32 == 0, lane % 32 == 31
    first, last = lane16 % 32 == 0, lane16 % 32 == 31
    dot = functools.partial(jnp.dot, preferred_element_type=F32)

    @pl.loop(0, 10)
    def _(i):
        for k in range(10):
            u = u_ref[i, k].astype(F32)
            before = jnp.where(lane >= 32, rolled(u, 32), 0.0)
            after = jnp.where(lane < 96, rolled(u, -32), 0.0)
            both = jnp.where(row >= 4, before, after)
            for g in range(3):
                if g == 0:
                    p, q = (jnp.where(first8, 0.0, rolled(v, 1)) for v in (u, both))
                elif g == 1:
                    p, q = u, both
                else:
                    p, q = (jnp.where(last8, 0.0, rolled(v, -1)) for v in (u, both))
                z[i, k, pl.ds(16 * g, 16)] = jnp.concatenate([p, q], 0).astype(BF)

    w1 = w1_ref[...]
    b1 = jnp.broadcast_to(b1_ref[...], (16, 128))

    def put(act, i, k, j, v):
        act[i, k, 1 + j] = v.astype(BF)
        if j == 7:
            act[i, k, 0] = jnp.where(lane16 >= 32, rolled(v, 32), 0.0).astype(BF)
        if j == 0:
            act[i, k, 9] = jnp.where(lane16 < 96, rolled(v, -32), 0.0).astype(BF)

    @pl.loop(0, 8)
    def _(i):
        @pl.loop(0, 4)
        def _(kk):
            cols = []
            for m in range(2):
                cols.append(jnp.concatenate(
                    [z[i + a, 2 * kk + m + e] for a in range(3) for e in range(3)], 0))
            y = dot(w1, jnp.concatenate(cols, 1))
            for m in range(2):
                k = 2 * kk + m
                gi, gk = 4 * s - 2 + i, 4 * t - 2 + k
                ok = (gi >= 0) & (gi < 4 * ns) & (gk >= 0) & (gk < 4 * nt)
                keep = jnp.where(ok, 1.0, 0.0)
                for j in range(8):
                    v = jnp.maximum(y[16 * j:16 * j + 16, 128 * m:128 * m + 128] + b1, 0.0) * keep
                    put(act1, i, k, j, v)

    w2 = w2_ref[...]
    b2 = jnp.broadcast_to(b2_ref[...], (16, 128))

    @pl.loop(0, 6)
    def _(i):
        @pl.loop(0, 6)
        def _(k):
            gi, gk = 4 * s - 1 + i, 4 * t - 1 + k
            ok = (gi >= 0) & (gi < 4 * ns) & (gk >= 0) & (gk < 4 * nt)
            keep = jnp.where(ok, 1.0, 0.0)
            for p in range(4):
                cols = []
                for m in range(2):
                    cols.append(jnp.concatenate(
                        [act1[i + a, k + e, 2 * p + m + b] for a in range(3) for e in range(3) for b in range(3)], 0))
                y = dot(w2, jnp.concatenate(cols, 1))
                for m in range(2):
                    h = slice(128 * m, 128 * m + 128)
                    v = (y[16:32, h] + jnp.where(first, 0.0, rolled(y[0:16, h], 1))
                         + jnp.where(last, 0.0, rolled(y[32:48, h], -1)) + b2)
                    put(act2, i, k, 2 * p + m, jnp.maximum(v, 0.0) * keep)

    w3 = w3_ref[...]
    b3 = b3_ref[0, 0]

    @pl.loop(0, 4)
    def _(i):
        @pl.loop(0, 2)
        def _(kk):
            y = None
            for a in range(3):
                cols = [jnp.concatenate([act2[i + a, 2 * kk + m + e].reshape(160, 128) for e in range(3)], 0)
                        for m in range(2)]
                part = dot(w3[:, 480 * a:480 * a + 480], jnp.concatenate(cols, 1))
                y = part if y is None else y + part
            for m in range(2):
                h = slice(128 * m, 128 * m + 128)
                v = (y[8:16, h] + jnp.where(first8, 0.0, rolled(y[0:8, h], 1))
                     + jnp.where(last8, 0.0, rolled(y[16:24, h], -1)) + b3)
                v = jnp.maximum(v, 0.0)
                o_ref[i, 2 * kk + m] = jnp.concatenate(
                    [v[:, 32 * q:32 * q + 32] for q in range(4)], 0).astype(BF)


def conv_call(ns, nt, u, w1, b1, w2, b2, w3, b3):
    vm = pl.BlockSpec(memory_space=pltpu.VMEM)
    return pl.pallas_call(
        functools.partial(conv_kernel, ns, nt),
        out_shape=jax.ShapeDtypeStruct((4, 4, 32, 32), BF),
        in_specs=[vm, vm, vm, vm, vm, vm, pl.BlockSpec(memory_space=pltpu.SMEM)],
        out_specs=vm,
        scratch_shapes=[
            pltpu.VMEM((10, 10, 48, 128), BF),
            pltpu.VMEM((8, 8, 10, 16, 128), BF),
            pltpu.VMEM((6, 6, 10, 16, 128), BF),
        ],
        compiler_params=pltpu.CompilerParams(vmem_limit_bytes=40 << 20),
    )(u, w1, b1, w2, b2, w3, b3)


def solution(mesh):
    ns, nt = mesh.shape["src"], mesh.shape["tgt"]

    def local(source, target, conv_one, bias_one, conv_two, bias_two, conv_three, bias_three):
        w1, w2, w3 = conv_weights(conv_one, conv_two, conv_three)
        vol = volume_call(ns, nt, source.reshape(128, -1), target.reshape(128, -1))
        out = conv_call(ns, nt, vol, w1, bias_one.reshape(16, 1), w2, bias_two.reshape(16, 1), w3,
                        bias_three.reshape(1, 1))
        return out[None]

    return jax.shard_map(
        local,
        mesh=mesh,
        in_specs=(P(None, "src", None, "tgt"), P(None, "tgt", None, "src")) + (P(),) * 6,
        out_specs=P(None, "src", "tgt", None, None),
        check_vma=False,
    )
```

profile of v0, /device:TPU:1, one launch (start us, length us, event | category | flops | bytes accessed | tf_op | source)
XLA Modules:
  0.0 62.6 jit_solution(17975595421521999046)
XLA Ops:
  0.0 0.7 %fusion.11 = (pred[1,8,16]{2,1,0:T(8,128)(4,1)S(1)}, pred[1,8,16]{2,1,0:T(8,128)(4,1)S(1)}, pred[1,8,16]{2,1,0:T(8,128)(4,1)S(1)}) fusion(s32[16]{0:T(128)} %constant.3.clone), kind=kLoop, calls=%fused_computation.17 | loop fusion | flops 640 | bytes 448 | tf_op jit(solution)/shard_map/eq | solution.py:185
  0.7 1.2 %convolution_bitcast_fusion.1 = bf16[8,16,3,3,3,16]{1,5,4,3,2,0:T(8,128)(2,1)S(1)} fusion(bf16[3,3,3,3,16]{4,3,2,1,0:T(4,128)(2,1)} %bitcast.31, pred[3,8,16,1,1,1]{2,1,0,5,4,3:T(8,128)(4,1)S(1)} %add_bitcast_fusion), kind=kOutput, calls=%fused_computation.1 | convolution fusion | flops 331776 | bytes 113568 | tf_op jit(solution)/shard_map/bjJ,abegd->jdaegJ/dot_general | solution.py:186
  1.9 0.2 copy.27
  2.1 0.6 reshape.209
  2.7 0.0 copy-start.3
  2.7 0.1 copy.32.w1_ref
  2.9 0.6 copy-done.3
  3.5 0.5 convolution_bitcast_fusion
  4.0 0.2 copy.31
  4.1 0.0 copy-start.2
  4.1 0.5 reshape.213.w3_ref
  4.6 0.5 copy-done.2
  5.1 0.3 copy.28
  5.4 0.0 copy-start
  5.4 0.2 reshape.211.w2_ref
  5.6 0.5 copy-done
  6.1 0.0 copy-done.1
  6.1 25.3 %shard_map.91.u_ref = bf16[10,10,8,128]{3,2,1,0:T(8,128)(2,1)S(1)} custom-call(bf16[128,32]{1,0:T(8,128)(2,1)S(1)} %bitcast.28, bf16[128,128]{1,0:T(8,128)(2,1)S(1)} %bitcast.29), custom_call_target="tpu_custom_call" | custom-call | tf_op jit(solution)/shard_map/pallas_call | solution.py:168
  31.4 0.0 copy-start.4
  31.4 0.6 %copy-done.4 = f32[16]{0:T(128)S(1)} copy-done((f32[16]{0:T(128)S(1)}, f32[16]{0:T(128)}, u32[]{:S(2)}) %copy-start.4) | copy-done | bytes 88
  32.1 0.1 copy.33.b1_ref
  32.2 0.7 %copy-done.5 = f32[16]{0:T(128)S(1)} copy-done((f32[16]{0:T(128)S(1)}, f32[16]{0:T(128)}, u32[]{:S(2)}) %copy-start.5) | copy-done | bytes 88
  32.8 0.1 copy.34.b2_ref
  33.6 29.1 %shard_map.92 = bf16[4,4,32,32]{3,2,1,0:T(8,128)(2,1)} custom-call(bf16[10,10,8,128]{3,2,1,0:T(8,128)(2,1)S(1)} %shard_map.91.u_ref, bf16[128,432]{1,0:T(8,128)(2,1)S(1)} %copy.32.w1_ref, f32[16,1]{1,0:T(8,128)S(1)} %copy.33.b1_ref, bf16[48,432]{1,0:T(8,128)(2,1)S(1)} %reshape.211.w2_ref, f32[16,1]{1,0:T(8,128)S(1)} %copy.34.b2_ref, ...), custom_call_target="tpu_custom_call" | custom-call | tf_op jit(solution)/shard_map/pallas_call | solution.py:297
  (6 shorter events, 0.0 us)
Async XLA Ops:
  2.7 0.7 %copy-start.3 = (bf16[3,3,3,3,16,1]{4,3,5,2,1,0:T(4,128)(2,1)S(1)}, bf16[3,3,3,3,16,1]{4,3,5,2,1,0:T(4,128)(2,1)}, u32[]{:S(2)}) copy-start(bf16[3,3,3,3,16,1]{4,3,5,2,1,0:T(4,128)(2,1)} %param.15) | copy-start | bytes 7780
  4.1 1.0 %copy-start.2 = (bf16[3,3,3,3,16,16]{5,4,3,2,1,0:T(8,128)(2,1)S(1)}, bf16[3,3,3,3,16,16]{5,4,3,2,1,0:T(8,128)(2,1)}, u32[]{:S(2)}) copy-start(bf16[3,3,3,3,16,16]{5,4,3,2,1,0:T(8,128)(2,1)} %param.13) | copy-start | bytes 124420
  5.4 0.8 %copy-start = (bf16[1,4,32,32]{3,2,1,0:T(8,128)(2,1)S(1)}, bf16[1,4,32,32]{3,2,1,0:T(8,128)(2,1)}, u32[]{:S(2)}) copy-start(bf16[1,4,32,32]{3,2,1,0:T(8,128)(2,1)} %param.9) | copy-start | bytes 24580
  5.4 0.8 %copy-start.1 = (bf16[1,4,32,128]{3,2,1,0:T(8,128)(2,1)S(1)}, bf16[1,4,32,128]{3,2,1,0:T(8,128)(2,1)}, u32[]{:S(2)}) copy-start(bf16[1,4,32,128]{3,2,1,0:T(8,128)(2,1)} %param.10) | copy-start | bytes 98308
  31.4 0.7 %copy-start.4 = (f32[16]{0:T(128)S(1)}, f32[16]{0:T(128)}, u32[]{:S(2)}) copy-start(f32[16]{0:T(128)} %param.12) | copy-start | bytes 196
  32.2 0.7 %copy-start.5 = (f32[16]{0:T(128)S(1)}, f32[16]{0:T(128)}, u32[]{:S(2)}) copy-start(f32[16]{0:T(128)} %param.14) | copy-start | bytes 196
where the time goes:
time: 63 us; the launch traced here: 62.6 us
  Pallas kernels  54.3 us (86%)
  local copies, waits for them, and re-layouts  5.09 us (8%)
  matrix products  1.71 us (3%)
  between operations  0.79 us (1%)
  other arithmetic  0.69 us (1%)
    pallas_call x1, Pallas kernels, conv_call(): pl.pallas_call(functools.partial(conv_kernel, ns, nt), out_shape=jax.Shap...  29.1 us
    pallas_call x1, Pallas kernels, volume_call(): pl.pallas_call(functools.partial(volume_kernel, ns, nt), out_shape=jax.Sh...  25.3 us
    unnamed x12, local copies, waits for them, and re-layouts  2.89 us

commit v1 on v0

v1 whole, which is shorter than its diff:
```python
import functools

import jax
import jax.numpy as jnp
from jax import lax
from jax.experimental import pallas as pl
from jax.experimental.pallas import tpu as pltpu
from jax.sharding import PartitionSpec as P

F32, BF = jnp.float32, jnp.bfloat16

MESH = pl.DeviceIdType.MESH
EPS = 1e-6
SIDES = [(ds, dt) for ds in (-1, 0, 1) for dt in (-1, 0, 1) if ds or dt]
NT = (((1,), (1,)), ((), ()))


def halo_span(d):
    if d == 0:
        return 0, 4, 3
    return (1, 3, 0) if d > 0 else (0, 3, 7)


def iota(shape, dim):
    return lax.broadcasted_iota(jnp.int32, shape, dim)


def hot(mask):
    return jnp.where(mask, 1.0, 0.0).astype(BF)


def make_w1(c1, flat, w1):
    flat[...] = jnp.zeros_like(flat)
    for n in range(27):
        flat[pl.ds(3 * n, 3), pl.ds(0, 16)] = c1[n].astype(F32)
    xt = flat[...].T[0:16, 0:96].astype(BF)
    n = iota((1, 432), 1)
    a, e, g, at = n // 144, (n // 48) % 3, (n // 16) % 3, n % 16
    at = jnp.where(at == 15, -1, jnp.where(at <= 8, at, 100))
    base = a * 27 + e * 3 + g
    r = iota((96, 432), 0)
    for j in range(8):
        b = at - j + 1
        key = jnp.where((b >= 0) & (b < 3), base + 9 * b, -1)
        w1[pl.ds(16 * j, 16)] = jnp.dot(xt, hot(r == key), preferred_element_type=F32).astype(BF)


def make_w2(c2, w2):
    eye = hot(iota((16, 16), 0) == iota((16, 16), 1))
    none = jnp.zeros((16, 16), BF)
    for i in range(2):
        for k in range(2):
            for g in range(3):
                pieces = []
                for up in range(4):
                    for across in range(4):
                        for b in range(3):
                            a, e = up - i, across - k
                            inside = 0 <= a < 3 and 0 <= e < 3
                            pieces.append(c2[((a * 3 + b) * 3 + e) * 3 + g] if inside else none)
                w2[pl.ds(((2 * i + k) * 3 + g) * 16, 16)] = lax.dot_general(
                    eye, jnp.concatenate(pieces, 0), NT, preferred_element_type=F32).astype(BF)


def make_w3(c3, flat, w3):
    flat[...] = jnp.zeros_like(flat)
    for n in range(27):
        flat[pl.ds(3 * n, 3), pl.ds(0, 16)] = c3[n].astype(F32)
    y = flat[pl.ds(0, 96), pl.ds(0, 16)].astype(BF)
    wide = jnp.dot(y, hot(iota((16, 256), 1) % 16 == iota((16, 256), 0)), preferred_element_type=F32).astype(BF)
    m = iota((48, 1), 0)
    b, slot = m // 16, (m % 16) // 4
    g = jnp.where(slot == 0, 1, jnp.where(slot == 1, 0, 2))
    r = iota((48, 96), 1)
    mm, nn = iota((48, 256), 0), iota((48, 256), 1)
    up, across = nn // 64 - (mm // 2) % 2, (nn // 16) % 4 - mm % 2
    total = jnp.zeros((48, 256), F32)
    for a in range(3):
        for e in range(3):
            key = jnp.where(slot < 3, a * 27 + b * 9 + e * 3 + g, -1)
            part = jnp.dot(hot(r == key), wide, preferred_element_type=F32)
            total = total + jnp.where((up == a) & (across == e), part, 0.0)
    w3[...] = total.astype(BF)


def inverse_root(v):
    r = lax.rsqrt(v)
    return r * (1.5 - 0.5 * v * r * r)


def column(row):
    square = jnp.where(iota((16, 16), 0) == iota((16, 16), 1), jnp.broadcast_to(row, (16, 16)), 0.0)
    return jnp.broadcast_to(jnp.sum(square, axis=1, keepdims=True), (16, 128))


def volume_kernel(ns, nt, src_hbm, tgt_hbm, c1_hbm, b1_hbm, c2_hbm, b2_hbm, c3_hbm, b3_ref,
                  vol, w1, w2, w3, bias,
                  src, gs, gt, own, c1, c2, c3, bs, flat1, flat3, load,
                  z_send, z_recv, y_send, y_recv, c_send, c_recv, x_send, x_recv, p_send, p_recv,
                  f_send, f_recv, h_send, h_recv):
    s, t = lax.axis_index("src"), lax.axis_index("tgt")
    nz, nx = nt // 4, ns // 2
    z, y, c = t // 4, (t // 2) % 2, t % 2
    x, h = s // 2, s % 2
    ch_s, ch_t = src.shape[-1], gt.shape[-1]

    fetches = [pltpu.make_async_copy(a, b, load.at[n]) for n, (a, b) in enumerate(
        [(src_hbm, src), (tgt_hbm, gt.at[s]), (c1_hbm, c1), (c2_hbm, c2), (c3_hbm, c3),
         (b1_hbm, bs.at[0]), (b2_hbm, bs.at[1])])]
    for f in fetches:
        f.start()

    vol[...] = jnp.zeros_like(vol)

    def tgt_at(zz, yy, cc):
        return 4 * zz + 2 * yy + cc

    def z_off(r):
        return lax.rem(z + r + nz, nz)

    def x_off(r):
        return lax.rem(x + r + nx, nx)

    def there(ds, dt):
        return (s + ds >= 0) & (s + ds < ns) & (t + dt >= 0) & (t + dt < nt)

    barrier = pltpu.get_barrier_semaphore()
    peers = [(s, tgt_at(z_off(r), y, c)) for r in range(1, nz)]
    peers += [(s, tgt_at(z, 1 - y, c)), (s, tgt_at(z, y, 1 - c))]
    peers += [(2 * x_off(r) + h, t) for r in range(1, nx)] + [(2 * x + 1 - h, t)]
    count = len(peers)
    for p in peers:
        pl.semaphore_signal(barrier, inc=1, device_id=p, device_id_type=MESH)
    for ds, dt in SIDES:
        count = count + jnp.where(there(ds, dt), 1, 0)

        @pl.when(there(ds, dt))
        def _():
            pl.semaphore_signal(barrier, inc=1, device_id=(s + ds, t + dt), device_id_type=MESH)

    fetches[0].wait()
    eye = hot(iota((ch_s, ch_s), 0) == iota((ch_s, ch_s), 1))
    gs[t] = lax.dot_general(eye, src[...], NT, preferred_element_type=F32).astype(BF)
    fetches[1].wait()
    pl.semaphore_wait(barrier, count)

    def remote(ref, sems, n, to):
        return pltpu.make_async_remote_copy(
            src_ref=ref, dst_ref=ref, send_sem=sems[0].at[n], recv_sem=sems[1].at[n],
            device_id=to, device_id_type=MESH)

    zs, ys, cs, xs, ps, fs = ((z_send, z_recv), (y_send, y_recv), (c_send, c_recv), (x_send, x_recv),
                              (p_send, p_recv), (f_send, f_recv))
    mate, twin, partner = (s, tgt_at(z, 1 - y, c)), (s, tgt_at(z, y, 1 - c)), (2 * x + 1 - h, t)

    def z_go(r):
        return remote(gs.at[t], zs, r - 1, (s, tgt_at(z_off(r), y, c)))

    def z_come(r):
        return remote(gs.at[tgt_at(z_off(-r), y, c)], zs, r - 1, mate)

    def y_go(q):
        return remote(gs.at[tgt_at(z_off(-q), y, c)], ys, q, mate)

    def y_come(q):
        return remote(gs.at[tgt_at(z_off(-q), 1 - y, c)], ys, q, mate)

    def c_go(q, w):
        return remote(gs.at[tgt_at(z_off(-q), y if w == 0 else 1 - y, c)], cs, 2 * q + w, twin)

    def c_come(q, w):
        return remote(gs.at[tgt_at(z_off(-q), y if w == 0 else 1 - y, 1 - c)], cs, 2 * q + w, twin)

    def x_go(r):
        return remote(gt.at[s], xs, r - 1, (2 * x_off(r) + h, t))

    def x_come(r):
        return remote(gt.at[2 * x_off(-r) + h], xs, r - 1, partner)

    p_go = remote(gt.at[s], ps, 0, partner)
    p_come = remote(gt.at[2 * x + 1 - h], ps, 0, partner)

    def f_go(r):
        return remote(gt.at[2 * x + 1 - h], fs, r - 1, (2 * x_off(r) + h, t))

    def f_come(r):
        return remote(gt.at[2 * x_off(-r) + 1 - h], fs, r - 1, partner)

    near = sorted(range(1, nz), key=lambda r: min(r, nz - r))
    for r in reversed(near):
        z_go(r).start()
    p_go.start()
    y_go(0).start()
    for r in range(1, nx):
        x_go(r).start()
    c_go(0, 0).start()

    for f in fetches[2:]:
        f.wait()
    make_w1(c1, flat1, w1)

    events = []
    for n, r in enumerate(near):
        d = min(r, nz - r)
        events.append((0.9 + 0.75 * d, "z", r))
        events.append((0.9 + 0.75 * d + 1.7, "y", r))
    events += [(1.7, "y", 0), (2.75, "p", 0), (2.5, "w", 0), (3.6, "w", 1), (4.0, "w", 2)]
    for _, kind, q in sorted(events):
        if kind == "z":
            z_come(q).wait_recv()
            y_go(q).start()
            c_go(q, 0).start()
        elif kind == "y":
            y_come(q).wait_recv()
            c_go(q, 1).start()
        elif kind == "p":
            p_come.wait_recv()
            for r in range(1, nx):
                f_go(r).start()
        elif q == 0:
            make_w3(c3, flat3, w3)
        elif q == 1:
            make_w2(c2, w2)
        else:
            bias[0] = column(bs[0])
            bias[1] = column(bs[1])
            bias[2] = jnp.full((16, 128), b3_ref[0, 0], F32)

    for r in range(1, nx):
        x_come(r).wait_recv()
    for r in range(1, nx):
        f_come(r).wait_recv()
    sq = None
    for n in range(ns):
        v = gt[n].astype(F32)
        sq = v * v if sq is None else sq + v * v
    inv_t = inverse_root(jnp.sum(sq, axis=1, keepdims=True) + EPS)

    for q in range(nz):
        for w in range(2):
            c_come(q, w).wait_recv()
    sq = None
    for n in range(nt):
        v = gs[n].astype(F32)
        v = v * v
        for q in range(ch_s // 8):
            p = v[8 * q:8 * q + 8]
            sq = p if sq is None else sq + p
    inv_s = inverse_root(jnp.sum(sq, axis=0, keepdims=True) + EPS)

    per = ch_t // ch_s
    acc = jnp.zeros((128, 128), F32)
    for n in range(ns):
        left = jnp.concatenate([gs[n * per + q] for q in range(per)], 0)
        left = (left.astype(F32) * inv_s).astype(BF)
        right = (gt[n].astype(F32) * inv_t).astype(BF)
        acc = acc + jnp.dot(right, left, preferred_element_type=F32)
    v = acc.T
    block = iota((8, 128), 1) // 32
    for i in range(4):
        for k in range(4):
            u = None
            for hi in range(4):
                w = v[32 * i + 8 * hi:32 * i + 8 * hi + 8]
                w = pltpu.roll(w, (32 * (hi - k)) % 128, 1) if hi != k else w
                u = w if u is None else jnp.where(block == hi, w, u)
            u = u.astype(BF)
            own[i, k] = u
            vol[3 + i, 3 + k] = u

    def halo(n, ds, dt):
        i0, ni, i1 = halo_span(ds)
        k0, nk, k1 = halo_span(dt)
        return pltpu.make_async_remote_copy(
            src_ref=own.at[pl.ds(i0, ni), pl.ds(k0, nk)], dst_ref=vol.at[pl.ds(i1, ni), pl.ds(k1, nk)],
            send_sem=h_send.at[n], recv_sem=h_recv.at[n], device_id=(s + ds, t + dt), device_id_type=MESH)

    for n, (ds, dt) in enumerate(SIDES):
        @pl.when(there(ds, dt))
        def _():
            halo(n, ds, dt).start()

    for r in near:
        z_go(r).wait_send()
    for q in range(nz):
        y_go(q).wait_send()
        for w in range(2):
            c_go(q, w).wait_send()
    p_go.wait_send()
    for r in range(1, nx):
        x_go(r).wait_send()
        f_go(r).wait_send()

    for n, (ds, dt) in enumerate(SIDES):
        @pl.when(there(-ds, -dt))
        def _():
            halo(n, ds, dt).wait_recv()

    for n, (ds, dt) in enumerate(SIDES):
        @pl.when(there(ds, dt))
        def _():
            halo(n, ds, dt).wait_send()


def rolled(x, by):
    return pltpu.roll(x, by % 128, 1)


def conv_kernel(ns, nt, u_ref, w1_ref, w2_ref, w3_ref, bias_ref, o_ref, z, act1, act2, fin):
    s, t = lax.axis_index("src"), lax.axis_index("tgt")
    lane = lax.broadcasted_iota(jnp.int32, (8, 128), 1)
    row = lax.broadcasted_iota(jnp.int32, (8, 128), 0)
    lane16 = lax.broadcasted_iota(jnp.int32, (16, 128), 1)
    first8, last8 = lane % 32 == 0, lane % 32 == 31
    first, last = lane16 % 32 == 0, lane16 % 32 == 31
    dot = functools.partial(jnp.dot, preferred_element_type=F32)

    @pl.loop(0, 10)
    def _(i):
        for k in range(10):
            u = u_ref[i, k].astype(F32)
            before = jnp.where(lane >= 32, rolled(u, 32), 0.0)
            after = jnp.where(lane < 96, rolled(u, -32), 0.0)
            both = jnp.where(row >= 4, before, after)
            for g in range(3):
                if g == 0:
                    p, q = (jnp.where(first8, 0.0, rolled(v, 1)) for v in (u, both))
                elif g == 1:
                    p, q = u, both
                else:
                    p, q = (jnp.where(last8, 0.0, rolled(v, -1)) for v in (u, both))
                z[i, k, pl.ds(16 * g, 16)] = jnp.concatenate([p, q], 0).astype(BF)

    w1 = w1_ref[...]
    b1 = bias_ref[0]

    def put(act, i, k, j, v):
        act[i, k, 1 + j] = v.astype(BF)
        if j == 7:
            act[i, k, 0] = jnp.where(lane16 >= 32, rolled(v, 32), 0.0).astype(BF)
        if j == 0:
            act[i, k, 9] = jnp.where(lane16 < 96, rolled(v, -32), 0.0).astype(BF)

    def kept(i, k, off):
        gi, gk = 4 * s - off + i, 4 * t - off + k
        ok = (gi >= 0) & (gi < 4 * ns) & (gk >= 0) & (gk < 4 * nt)
        return jnp.where(ok, 1.0, 0.0)

    if 3 >= 1:
        @pl.loop(0, 8)
        def _(i):
            for kk in range(4):
                cols = []
                for m in range(2):
                    cols.append(jnp.concatenate(
                        [z[i + a, 2 * kk + m + e] for a in range(3) for e in range(3)], 0))
                y = dot(w1, jnp.concatenate(cols, 1))
                for m in range(2):
                    k = 2 * kk + m
                    keep = kept(i, k, 2)
                    for j in range(8):
                        v = jnp.maximum(y[16 * j:16 * j + 16, 128 * m:128 * m + 128] + b1, 0.0) * keep
                        put(act1, i, k, j, v)

    b2 = bias_ref[1]
    if 3 >= 2:
        @pl.loop(0, 3)
        def _(ii):
            for kk in range(3):
                for p in range(4):
                    cols = []
                    for m in range(2):
                        cols.append(jnp.concatenate(
                            [act1[2 * ii + a, 2 * kk + e, 2 * p + m + b]
                             for a in range(4) for e in range(4) for b in range(3)], 0))
                    y = dot(w2_ref[...], jnp.concatenate(cols, 1))
                    for di in range(2):
                        for dk in range(2):
                            i, k = 2 * ii + di, 2 * kk + dk
                            keep = kept(i, k, 1)
                            r = 48 * (2 * di + dk)
                            for m in range(2):
                                h = slice(128 * m, 128 * m + 128)
                                v = (y[r + 16:r + 32, h] + jnp.where(first, 0.0, rolled(y[r:r + 16, h], 1))
                                     + jnp.where(last, 0.0, rolled(y[r + 32:r + 48, h], -1)) + b2)
                                put(act2, i, k, 2 * p + m, jnp.maximum(v, 0.0) * keep)

    w3 = w3_ref[...]
    b3 = bias_ref[2, pl.ds(0, 8)]
    if 3 >= 3:
        for ii in range(2):
            for kk in range(2):
                per_col = []
                for q in range(5):
                    y = dot(w3, jnp.concatenate([jnp.concatenate(
                        [act2[2 * ii + a, 2 * kk + e, 2 * q + m] for a in range(4) for e in range(4)], 0)
                        for m in range(2)], 1))
                    per_col += [y[:, 0:128], y[:, 128:256]]
                buf = fin.at[2 * ii + kk]
                for j in range(8):
                    v = per_col[j][0:16] + per_col[j + 1][16:32] + per_col[j + 2][32:48]
                    left = pltpu.roll(jnp.where(first8, 0.0, rolled(v[0:8], 1)), 4, 0)
                    v = v[0:8] + left + jnp.where(last8, 0.0, rolled(v[8:16], -1)) + b3
                    buf[pl.ds(8 * j, 8)] = jnp.maximum(v, 0.0)
                for di in range(2):
                    for dk in range(2):
                        v = buf[pl.ds(2 * di + dk, 8, stride=8), :]
                        o_ref[2 * ii + di, 2 * kk + dk] = jnp.concatenate(
                            [v[:, 32 * q:32 * q + 32] for q in range(4)], 0).astype(BF)


def whole_kernel(ns, nt, *refs):
    given, (out, vol, w1, w2, w3, bias, z, act1, act2, fin), rest = refs[:8], refs[8:18], refs[18:]
    volume_kernel(ns, nt, *given, vol, w1, w2, w3, bias, *rest)
    conv_kernel(ns, nt, vol, w1, w2, w3, bias, out, z, act1, act2, fin)


def whole_call(ns, nt, *given):
    src, tgt = given[:2]
    hbm = pl.BlockSpec(memory_space=pl.ANY)
    vmem, dma = pltpu.VMEM, pltpu.SemaphoreType.DMA
    pairs = [nt // 4 - 1, nt // 4, nt // 2, ns // 2 - 1, 1, ns // 2 - 1, 8]
    return pl.pallas_call(
        functools.partial(whole_kernel, ns, nt),
        out_shape=jax.ShapeDtypeStruct((4, 4, 32, 32), BF),
        in_specs=[hbm] * 7 + [pl.BlockSpec(memory_space=pltpu.SMEM)],
        out_specs=pl.BlockSpec(memory_space=pltpu.VMEM),
        scratch_shapes=[
            vmem((10, 10, 8, 128), BF), vmem((128, 432), BF), vmem((192, 768), BF), vmem((48, 256), BF),
            vmem((3, 16, 128), F32),
            vmem((10, 10, 48, 128), BF), vmem((8, 8, 10, 16, 128), BF), vmem((6, 6, 10, 16, 128), BF),
            vmem((4, 64, 128), F32),
            vmem(src.shape, BF), vmem((nt, src.shape[-1], 128), BF), vmem((ns, 128, tgt.shape[-1]), BF),
            vmem((4, 4, 8, 128), BF),
            vmem((27, 3, 16), BF), vmem((81, 16, 16), BF), vmem((27, 3, 16), BF), vmem((2, 1, 16), F32),
            vmem((128, 128), F32), vmem((128, 128), F32),
            dma((7,)),
        ] + [dma((max(n, 1),)) for n in pairs for _ in range(2)],
        compiler_params=pltpu.CompilerParams(
            collective_id=0, has_side_effects=True, vmem_limit_bytes=65000000),
    )(*given)


def solution(mesh):
    ns, nt = mesh.shape["src"], mesh.shape["tgt"]

    def local(source, target, conv_one, bias_one, conv_two, bias_two, conv_three, bias_three):
        out = whole_call(
            ns, nt, source.reshape(128, -1), target.reshape(128, -1),
            conv_one.reshape(27, 3, 16), bias_one.reshape(1, 16), conv_two.reshape(81, 16, 16),
            bias_two.reshape(1, 16), conv_three.reshape(27, 3, 16), bias_three.reshape(1, 1))
        return out[None]

    return jax.shard_map(
        local,
        mesh=mesh,
        in_specs=(P(None, "src", None, "tgt"), P(None, "tgt", None, "src")) + (P(),) * 6,
        out_specs=P(None, "src", "tgt", None, None),
        check_vma=False,
    )
```

time: 63 us -> 37.8 us (0.60)
  Pallas kernels: 54.3 us -> 35.4 us
  local copies, waits for them, and re-layouts: 5.09 us -> 1.57 us
  matrix products: 1.71 us -> 0 us
  other arithmetic: 0.69 us -> 0 us
    pallas_call x2 -> x1, Pallas kernels: 54.3 us -> 35.4 us  [whole_call(): pl.pallas_call(functools.partial(whole_kernel, ns, nt), out_shape=jax.Sha...]
    dot_general x2 -> x0, matrix products: 1.71 us -> none  [the longest x1 1.23 us: conv_weights(): jnp.einsum('bjJ,abegd->jdaegJ', hot1, conv_one[:, :, :, :, 0, :])]
    reshape x6 -> x0, local copies, waits for them, and re-layouts: 1.57 us -> none  [the longest x2 0.68 us: conv_weights(): jnp.einsum('bjJ,abegd->jdaegJ', hot1, conv_one[:, :, :, :, 0, :])]
    unnamed x12 -> x1, local copies, waits for them, and re-layouts: 2.89 us -> 1.57 us
    eq x2 -> x0, other arithmetic: 0.67 us -> none  [the longest x1 0.66 us: conv_weights(): hot1 = jnp.stack([at - j + 1 == b for b in range(3)]).astype(BF)]
    transpose x3 -> x0, local copies, waits for them, and re-layouts: 0.64 us -> none  [the longest x1 0.25 us: conv_weights(): w2 = jnp.transpose(conv_two, (3, 5, 0, 2, 1, 4)).reshape(48, 432)]
where the time goes in v1:
time: 37.8 us; the launch traced here: 37.7 us
  Pallas kernels  35.4 us (94%)
  local copies, waits for them, and re-layouts  1.57 us (4%)
  between operations  0.66 us (2%)
    pallas_call x1, Pallas kernels, whole_call(): pl.pallas_call(functools.partial(whole_kernel, ns, nt), out_shape=jax.Sha...  35.4 us
    unnamed x1, local copies, waits for them, and re-layouts  1.57 us

profile of v1, /device:TPU:1, one launch (start us, length us, event | category | flops | bytes accessed | tf_op | source)
XLA Modules:
  0.0 37.7 jit_solution(16365677897509108574)
XLA Ops:
  0.7 35.4 %shard_map.82 = bf16[4,4,32,32]{3,2,1,0:T(8,128)(2,1)} custom-call(bf16[128,32]{1,0:T(8,128)(2,1)} %bitcast.12, bf16[128,128]{1,0:T(8,128)(2,1)} %bitcast.13, bf16[27,3,16]{2,1,0:T(4,128)(2,1)} %bitcast.14, f32[1,16]{1,0:T(1,128)} %bitcast.16, bf16[81,16,16]{2,1,0:T(8,128)(2,1)} %bitcast.11, f32[1,16]{1,0:T(1,128)} %bitcast.17, bf16[27,3,16]{2,1,0:T(4,128)(2,1)} %bitcast.15, ...), custom_call_target="tpu_custom_call" | custom-call | tf_op jit(solution)/shard_map/pallas_call | solution.py:423
  36.1 1.6 %copy.11 = bf16[1,4,4,32,32]{4,3,2,1,0:T(8,128)(2,1)} copy(bf16[1,4,4,32,32]{4,3,2,1,0:T(8,128)(2,1)} %bitcast.10) | data formatting | bytes 65536

commit v2 on v1

--- a/solution.py
+++ b/solution.py
@@ -93,7 +93,7 @@
     return jnp.broadcast_to(jnp.sum(square, axis=1, keepdims=True), (16, 128))
 
 
-def volume_kernel(ns, nt, src_hbm, tgt_hbm, c1_hbm, b1_hbm, c2_hbm, b2_hbm, c3_hbm, b3_ref,
+def volume_kernel(ns, nt, meanwhile, src_hbm, tgt_hbm, c1_hbm, b1_hbm, c2_hbm, b2_hbm, c3_hbm, b3_ref,
                   vol, w1, w2, w3, bias,
                   src, gs, gt, own, c1, c2, c3, bs, flat1, flat3, load,
                   z_send, z_recv, y_send, y_recv, c_send, c_recv, x_send, x_recv, p_send, p_recv,
@@ -126,7 +126,7 @@
 
     barrier = pltpu.get_barrier_semaphore()
     peers = [(s, tgt_at(z_off(r), y, c)) for r in range(1, nz)]
-    peers += [(s, tgt_at(z, 1 - y, c)), (s, tgt_at(z, y, 1 - c))]
+    peers += [(s, tgt_at(z, 1 - y, c)), (s, tgt_at(z, 1 - y, 1 - c)), (s, tgt_at(z, y, 1 - c))]
     peers += [(2 * x_off(r) + h, t) for r in range(1, nx)] + [(2 * x + 1 - h, t)]
     count = len(peers)
     for p in peers:
@@ -152,6 +152,7 @@
     zs, ys, cs, xs, ps, fs = ((z_send, z_recv), (y_send, y_recv), (c_send, c_recv), (x_send, x_recv),
                               (p_send, p_recv), (f_send, f_recv))
     mate, twin, partner = (s, tgt_at(z, 1 - y, c)), (s, tgt_at(z, y, 1 - c)), (2 * x + 1 - h, t)
+    across = (s, tgt_at(z, 1 - y, 1 - c))
 
     def z_go(r):
         return remote(gs.at[t], zs, r - 1, (s, tgt_at(z_off(r), y, c)))
@@ -166,7 +167,7 @@
         return remote(gs.at[tgt_at(z_off(-q), 1 - y, c)], ys, q, mate)
 
     def c_go(q, w):
-        return remote(gs.at[tgt_at(z_off(-q), y if w == 0 else 1 - y, c)], cs, 2 * q + w, twin)
+        return remote(gs.at[tgt_at(z_off(-q), y, c)], cs, 2 * q + w, twin if w == 0 else across)
 
     def c_come(q, w):
         return remote(gs.at[tgt_at(z_off(-q), y if w == 0 else 1 - y, 1 - c)], cs, 2 * q + w, twin)
@@ -191,6 +192,7 @@
         z_go(r).start()
     p_go.start()
     y_go(0).start()
+    c_go(0, 1).start()
     for r in range(1, nx):
         x_go(r).start()
     c_go(0, 0).start()
@@ -203,16 +205,13 @@
     for n, r in enumerate(near):
         d = min(r, nz - r)
         events.append((0.9 + 0.75 * d, "z", r))
-        events.append((0.9 + 0.75 * d + 1.7, "y", r))
-    events += [(1.7, "y", 0), (2.75, "p", 0), (2.5, "w", 0), (3.6, "w", 1), (4.0, "w", 2)]
+    events += [(2.75, "p", 0), (2.5, "w", 0), (3.6, "w", 1), (4.0, "w", 2)]
     for _, kind, q in sorted(events):
         if kind == "z":
             z_come(q).wait_recv()
             y_go(q).start()
+            c_go(q, 1).start()
             c_go(q, 0).start()
-        elif kind == "y":
-            y_come(q).wait_recv()
-            c_go(q, 1).start()
         elif kind == "p":
             p_come.wait_recv()
             for r in range(1, nx):
@@ -237,6 +236,7 @@
     inv_t = inverse_root(jnp.sum(sq, axis=1, keepdims=True) + EPS)
 
     for q in range(nz):
+        y_come(q).wait_recv()
         for w in range(2):
             c_come(q, w).wait_recv()
     sq = None
@@ -280,6 +280,17 @@
         def _():
             halo(n, ds, dt).start()
 
+    def arrived(wanted):
+        for n, (ds, dt) in enumerate(SIDES):
+            if wanted(ds):
+                @pl.when(there(-ds, -dt))
+                def _():
+                    halo(n, ds, dt).wait_recv()
+
+    arrived(lambda ds: ds == 0)
+    meanwhile()
+    arrived(lambda ds: ds != 0)
+
     for r in near:
         z_go(r).wait_send()
     for q in range(nz):
@@ -292,11 +303,6 @@
         f_go(r).wait_send()
 
     for n, (ds, dt) in enumerate(SIDES):
-        @pl.when(there(-ds, -dt))
-        def _():
-            halo(n, ds, dt).wait_recv()
-
-    for n, (ds, dt) in enumerate(SIDES):
         @pl.when(there(ds, dt))
         def _():
             halo(n, ds, dt).wait_send()
@@ -306,7 +312,7 @@
     return pltpu.roll(x, by % 128, 1)
 
 
-def conv_kernel(ns, nt, u_ref, w1_ref, w2_ref, w3_ref, bias_ref, o_ref, z, act1, act2, fin):
+def conv_stages(ns, nt, u_ref, w1_ref, w2_ref, w3_ref, bias_ref, o_ref, z, act1, act2, fin):
     s, t = lax.axis_index("src"), lax.axis_index("tgt")
     lane = lax.broadcasted_iota(jnp.int32, (8, 128), 1)
     row = lax.broadcasted_iota(jnp.int32, (8, 128), 0)
@@ -315,24 +321,23 @@
     first, last = lane16 % 32 == 0, lane16 % 32 == 31
     dot = functools.partial(jnp.dot, preferred_element_type=F32)
 
-    @pl.loop(0, 10)
-    def _(i):
-        for k in range(10):
-            u = u_ref[i, k].astype(F32)
-            before = jnp.where(lane >= 32, rolled(u, 32), 0.0)
-            after = jnp.where(lane < 96, rolled(u, -32), 0.0)
-            both = jnp.where(row >= 4, before, after)
-            for g in range(3):
-                if g == 0:
-                    p, q = (jnp.where(first8, 0.0, rolled(v, 1)) for v in (u, both))
-                elif g == 1:
-                    p, q = u, both
-                else:
-                    p, q = (jnp.where(last8, 0.0, rolled(v, -1)) for v in (u, both))
-                z[i, k, pl.ds(16 * g, 16)] = jnp.concatenate([p, q], 0).astype(BF)
-
-    w1 = w1_ref[...]
-    b1 = bias_ref[0]
+    def pieces(lo, hi):
+        @pl.loop(lo, hi)
+        def _(i):
+            for k in range(10):
+                u = u_ref[i, k].astype(F32)
+                before = jnp.where(lane >= 32, rolled(u, 32), 0.0)
+                after = jnp.where(lane < 96, rolled(u, -32), 0.0)
+                both = jnp.where(row >= 4, before, after)
+                for g in range(3):
+                    if g == 0:
+                        p, q = (jnp.where(first8, 0.0, rolled(v, 1)) for v in (u, both))
+                    elif g == 1:
+                        p, q = u, both
+                    else:
+                        p, q = (jnp.where(last8, 0.0, rolled(v, -1)) for v in (u, both))
+                    z[i, k, pl.ds(16 * g, 16)] = jnp.concatenate([p, q], 0).astype(BF)
+
 
     def put(act, i, k, j, v):
         act[i, k, 1 + j] = v.astype(BF)
@@ -346,8 +351,10 @@
         ok = (gi >= 0) & (gi < 4 * ns) & (gk >= 0) & (gk < 4 * nt)
         return jnp.where(ok, 1.0, 0.0)
 
-    if 3 >= 1:
-        @pl.loop(0, 8)
+    def layer_one(lo, hi):
+        w1, b1 = w1_ref[...], bias_ref[0]
+
+        @pl.loop(lo, hi)
         def _(i):
             for kk in range(4):
                 cols = []
@@ -362,8 +369,8 @@
                         v = jnp.maximum(y[16 * j:16 * j + 16, 128 * m:128 * m + 128] + b1, 0.0) * keep
                         put(act1, i, k, j, v)
 
-    b2 = bias_ref[1]
-    if 3 >= 2:
+    def rest():
+        b2 = bias_ref[1]
         @pl.loop(0, 3)
         def _(ii):
             for kk in range(3):
@@ -385,9 +392,8 @@
                                      + jnp.where(last, 0.0, rolled(y[r + 32:r + 48, h], -1)) + b2)
                                 put(act2, i, k, 2 * p + m, jnp.maximum(v, 0.0) * keep)
 
-    w3 = w3_ref[...]
-    b3 = bias_ref[2, pl.ds(0, 8)]
-    if 3 >= 3:
+        w3 = w3_ref[...]
+        b3 = bias_ref[2, pl.ds(0, 8)]
         for ii in range(2):
             for kk in range(2):
                 per_col = []
@@ -408,11 +414,23 @@
                         o_ref[2 * ii + di, 2 * kk + dk] = jnp.concatenate(
                             [v[:, 32 * q:32 * q + 32] for q in range(4)], 0).astype(BF)
 
+    return pieces, layer_one, rest
+
 
 def whole_kernel(ns, nt, *refs):
     given, (out, vol, w1, w2, w3, bias, z, act1, act2, fin), rest = refs[:8], refs[8:18], refs[18:]
-    volume_kernel(ns, nt, *given, vol, w1, w2, w3, bias, *rest)
-    conv_kernel(ns, nt, vol, w1, w2, w3, bias, out, z, act1, act2, fin)
+    pieces, layer_one, others = conv_stages(ns, nt, vol, w1, w2, w3, bias, out, z, act1, act2, fin)
+
+    def meanwhile():
+        pieces(3, 7)
+        layer_one(3, 5)
+
+    volume_kernel(ns, nt, meanwhile, *given, vol, w1, w2, w3, bias, *rest)
+    pieces(0, 3)
+    pieces(7, 10)
+    layer_one(0, 3)
+    layer_one(5, 8)
+    others()
 
 
 def whole_call(ns, nt, *given):
@@ -422,7 +440,7 @@
     pairs = [nt // 4 - 1, nt // 4, nt // 2, ns // 2 - 1, 1, ns // 2 - 1, 8]
     return pl.pallas_call(
         functools.partial(whole_kernel, ns, nt),
-        out_shape=jax.ShapeDtypeStruct((4, 4, 32, 32), BF),
+        out_shape=pltpu.VMEM((4, 4, 32, 32), BF),
         in_specs=[hbm] * 7 + [pl.BlockSpec(memory_space=pltpu.SMEM)],
         out_specs=pl.BlockSpec(memory_space=pltpu.VMEM),
         scratch_shapes=[

time: 37.8 us -> 34.1 us (0.902)
  Pallas kernels: 35.4 us -> 32.7 us
  local copies, waits for them, and re-layouts: 1.57 us -> 0.66 us
    pallas_call x1, Pallas kernels: 35.4 us -> 32.7 us  [whole_call(): pl.pallas_call(functools.partial(whole_kernel, ns, nt), out_shape=pltpu.V...]
    unnamed x1, local copies, waits for them, and re-layouts: 1.57 us -> 0.66 us
where the time goes in v2:
time: 34.1 us; the launch traced here: 34 us
  Pallas kernels  32.7 us (96%)
  local copies, waits for them, and re-layouts  0.66 us (2%)
  between operations  0.66 us (2%)
    pallas_call x1, Pallas kernels, whole_call(): pl.pallas_call(functools.partial(whole_kernel, ns, nt), out_shape=pltpu.V...  32.7 us

profile of v2, /device:TPU:1, one launch (start us, length us, event | category | flops | bytes accessed | tf_op | source)
XLA Modules:
  0.0 34.0 jit_solution(17605042915795487215)
XLA Ops:
  0.7 32.7 %shard_map.82 = bf16[4,4,32,32]{3,2,1,0:T(8,128)(2,1)S(1)} custom-call(bf16[128,32]{1,0:T(8,128)(2,1)} %bitcast.12, bf16[128,128]{1,0:T(8,128)(2,1)} %bitcast.13, bf16[27,3,16]{2,1,0:T(4,128)(2,1)} %bitcast.14, f32[1,16]{1,0:T(1,128)} %bitcast.16, bf16[81,16,16]{2,1,0:T(8,128)(2,1)} %bitcast.11, f32[1,16]{1,0:T(1,128)} %bitcast.17, ...), custom_call_target="tpu_custom_call" | custom-call | tf_op jit(solution)/shard_map/pallas_call | solution.py:441
  33.3 0.7 %copy.10 = bf16[1,4,4,32,32]{4,3,2,1,0:T(8,128)(2,1)} copy(bf16[1,4,4,32,32]{4,3,2,1,0:T(8,128)(2,1)S(1)} %bitcast.10) | data formatting | bytes 65536

commit v3 on v2

--- a/solution.py
+++ b/solution.py
@@ -34,15 +34,21 @@
     for n in range(27):
         flat[pl.ds(3 * n, 3), pl.ds(0, 16)] = c1[n].astype(F32)
     xt = flat[...].T[0:16, 0:96].astype(BF)
-    n = iota((1, 432), 1)
-    a, e, g, at = n // 144, (n // 48) % 3, (n // 16) % 3, n % 16
-    at = jnp.where(at == 15, -1, jnp.where(at <= 8, at, 100))
-    base = a * 27 + e * 3 + g
-    r = iota((96, 432), 0)
-    for j in range(8):
-        b = at - j + 1
-        key = jnp.where((b >= 0) & (b < 3), base + 9 * b, -1)
-        w1[pl.ds(16 * j, 16)] = jnp.dot(xt, hot(r == key), preferred_element_type=F32).astype(BF)
+    n = iota((1, 192), 1)
+    a, across, half, at = n // 64, (n // 16) % 4, (n % 16) // 8, n % 8
+    r = iota((96, 192), 0)
+    for q in range(3):
+        d = (at - (3 * q - 1) + 8) % 8
+        from_ = jnp.where(d <= 4, d, jnp.where(half == 0, d - 5, d - 2))
+        g = jnp.where(d <= 4, 2 * half, 1)
+        for j in range(3 if q < 2 else 2):
+            b = from_ - j
+            for k in range(2):
+                e = across - k
+                inside = (from_ <= 4) & (b >= 0) & (b < 3) & (e >= 0) & (e < 3)
+                key = jnp.where(inside, a * 27 + b * 9 + e * 3 + g, -1)
+                w1[pl.ds(96 * q + 32 * j + 16 * k, 16)] = jnp.dot(
+                    xt, hot(r == key), preferred_element_type=F32).astype(BF)
 
 
 def make_w2(c2, w2):
@@ -172,25 +178,34 @@
     def c_come(q, w):
         return remote(gs.at[tgt_at(z_off(-q), y if w == 0 else 1 - y, 1 - c)], cs, 2 * q + w, twin)
 
+    def half(ref, m):
+        return ref.at[pl.ds(64 * m, 64)]
+
     def x_go(r):
         return remote(gt.at[s], xs, r - 1, (2 * x_off(r) + h, t))
 
     def x_come(r):
         return remote(gt.at[2 * x_off(-r) + h], xs, r - 1, partner)
 
-    p_go = remote(gt.at[s], ps, 0, partner)
-    p_come = remote(gt.at[2 * x + 1 - h], ps, 0, partner)
-
-    def f_go(r):
-        return remote(gt.at[2 * x + 1 - h], fs, r - 1, (2 * x_off(r) + h, t))
-
-    def f_come(r):
-        return remote(gt.at[2 * x_off(-r) + 1 - h], fs, r - 1, partner)
+    def p_go(m):
+        return remote(half(gt.at[s], m), ps, m, partner)
+
+    def p_come(m):
+        return remote(half(gt.at[2 * x + 1 - h], m), ps, m, partner)
+
+    def f_go(r, m):
+        return remote(half(gt.at[2 * x + 1 - h], m), fs, 2 * r - 2 + m, (2 * x_off(r) + h, t))
+
+    def f_come(r, m):
+        return remote(half(gt.at[2 * x_off(-r) + 1 - h], m), fs, 2 * r - 2 + m, partner)
+
+    far = sorted(range(1, nx), key=lambda r: -min(r, nx - r))
 
     near = sorted(range(1, nz), key=lambda r: min(r, nz - r))
     for r in reversed(near):
         z_go(r).start()
-    p_go.start()
+    p_go(0).start()
+    p_go(1).start()
     y_go(0).start()
     c_go(0, 1).start()
     for r in range(1, nx):
@@ -205,7 +220,7 @@
     for n, r in enumerate(near):
         d = min(r, nz - r)
         events.append((0.9 + 0.75 * d, "z", r))
-    events += [(2.75, "p", 0), (2.5, "w", 0), (3.6, "w", 1), (4.0, "w", 2)]
+    events += [(2.6, "p", 0), (2.8, "p", 1), (2.5, "w", 0), (3.6, "w", 1), (4.0, "w", 2)]
     for _, kind, q in sorted(events):
         if kind == "z":
             z_come(q).wait_recv()
@@ -213,9 +228,9 @@
             c_go(q, 1).start()
             c_go(q, 0).start()
         elif kind == "p":
-            p_come.wait_recv()
-            for r in range(1, nx):
-                f_go(r).start()
+            p_come(q).wait_recv()
+            for r in far:
+                f_go(r, q).start()
         elif q == 0:
             make_w3(c3, flat3, w3)
         elif q == 1:
@@ -228,7 +243,8 @@
     for r in range(1, nx):
         x_come(r).wait_recv()
     for r in range(1, nx):
-        f_come(r).wait_recv()
+        for m in range(2):
+            f_come(r, m).wait_recv()
     sq = None
     for n in range(ns):
         v = gt[n].astype(F32)
@@ -297,10 +313,12 @@
         y_go(q).wait_send()
         for w in range(2):
             c_go(q, w).wait_send()
-    p_go.wait_send()
+    p_go(0).wait_send()
+    p_go(1).wait_send()
     for r in range(1, nx):
         x_go(r).wait_send()
-        f_go(r).wait_send()
+        f_go(r, 0).wait_send()
+        f_go(r, 1).wait_send()
 
     for n, (ds, dt) in enumerate(SIDES):
         @pl.when(there(ds, dt))
@@ -328,16 +346,13 @@
                 u = u_ref[i, k].astype(F32)
                 before = jnp.where(lane >= 32, rolled(u, 32), 0.0)
                 after = jnp.where(lane < 96, rolled(u, -32), 0.0)
-                both = jnp.where(row >= 4, before, after)
-                for g in range(3):
-                    if g == 0:
-                        p, q = (jnp.where(first8, 0.0, rolled(v, 1)) for v in (u, both))
-                    elif g == 1:
-                        p, q = u, both
-                    else:
-                        p, q = (jnp.where(last8, 0.0, rolled(v, -1)) for v in (u, both))
-                    z[i, k, pl.ds(16 * g, 16)] = jnp.concatenate([p, q], 0).astype(BF)
-
+                for q, v in enumerate((jnp.where(row == 7, before, u), u, jnp.where(row == 0, after, u))):
+                    left = jnp.where(first8, 0.0, rolled(v, 1))
+                    right = jnp.where(last8, 0.0, rolled(v, -1))
+                    own = (row - (3 * q - 1) + 8) % 8 <= 4
+                    z[i, k, pl.ds(16 * q, 16)] = jnp.concatenate([
+                        jnp.where(own, left, pltpu.roll(v, 5, 0)),
+                        jnp.where(own, right, pltpu.roll(v, 2, 0))], 0).astype(BF)
 
     def put(act, i, k, j, v):
         act[i, k, 1 + j] = v.astype(BF)
@@ -352,22 +367,26 @@
         return jnp.where(ok, 1.0, 0.0)
 
     def layer_one(lo, hi):
-        w1, b1 = w1_ref[...], bias_ref[0]
+        b1 = bias_ref[0]
 
         @pl.loop(lo, hi)
         def _(i):
-            for kk in range(4):
-                cols = []
-                for m in range(2):
-                    cols.append(jnp.concatenate(
-                        [z[i + a, 2 * kk + m + e] for a in range(3) for e in range(3)], 0))
-                y = dot(w1, jnp.concatenate(cols, 1))
-                for m in range(2):
-                    k = 2 * kk + m
-                    keep = kept(i, k, 2)
-                    for j in range(8):
-                        v = jnp.maximum(y[16 * j:16 * j + 16, 128 * m:128 * m + 128] + b1, 0.0) * keep
-                        put(act1, i, k, j, v)
+            for kk in range(2):
+                for q in range(3):
+                    cols = []
+                    for m in range(2):
+                        cols.append(jnp.concatenate(
+                            [z[i + a, 4 * kk + 2 * m + e, pl.ds(16 * q, 16)] for a in range(3) for e in range(4)], 0))
+                    wide = 3 if q < 2 else 2
+                    y = dot(w1_ref[pl.ds(96 * q, 32 * wide)], jnp.concatenate(cols, 1))
+                    for m in range(2):
+                        for dk in range(2):
+                            k = 4 * kk + 2 * m + dk
+                            keep = kept(i, k, 2)
+                            for j in range(wide):
+                                r = 32 * j + 16 * dk
+                                v = jnp.maximum(y[r:r + 16, 128 * m:128 * m + 128] + b1, 0.0) * keep
+                                put(act1, i, k, 3 * q + j, v)
 
     def rest():
         b2 = bias_ref[1]
@@ -437,14 +456,14 @@
     src, tgt = given[:2]
     hbm = pl.BlockSpec(memory_space=pl.ANY)
     vmem, dma = pltpu.VMEM, pltpu.SemaphoreType.DMA
-    pairs = [nt // 4 - 1, nt // 4, nt // 2, ns // 2 - 1, 1, ns // 2 - 1, 8]
+    pairs = [nt // 4 - 1, nt // 4, nt // 2, ns // 2 - 1, 2, ns - 2, 8]
     return pl.pallas_call(
         functools.partial(whole_kernel, ns, nt),
         out_shape=pltpu.VMEM((4, 4, 32, 32), BF),
         in_specs=[hbm] * 7 + [pl.BlockSpec(memory_space=pltpu.SMEM)],
         out_specs=pl.BlockSpec(memory_space=pltpu.VMEM),
         scratch_shapes=[
-            vmem((10, 10, 8, 128), BF), vmem((128, 432), BF), vmem((192, 768), BF), vmem((48, 256), BF),
+            vmem((10, 10, 8, 128), BF), vmem((256, 192), BF), vmem((192, 768), BF), vmem((48, 256), BF),
             vmem((3, 16, 128), F32),
             vmem((10, 10, 48, 128), BF), vmem((8, 8, 10, 16, 128), BF), vmem((6, 6, 10, 16, 128), BF),
             vmem((4, 64, 128), F32),

time: 34.1 us -> 32.9 us (0.965)
  Pallas kernels: 32.7 us -> 31.5 us
    pallas_call x1, Pallas kernels: 32.7 us -> 31.5 us  [whole_call(): pl.pallas_call(functools.partial(whole_kernel, ns, nt), out_shape=pltpu.V...]
where the time goes in v3:
time: 32.9 us; the launch traced here: 32.8 us
  Pallas kernels  31.5 us (96%)
  local copies, waits for them, and re-layouts  0.66 us (2%)
  between operations  0.66 us (2%)
    pallas_call x1, Pallas kernels, whole_call(): pl.pallas_call(functools.partial(whole_kernel, ns, nt), out_shape=pltpu.V...  31.5 us

profile of v3, /device:TPU:1, one launch (start us, length us, event | category | flops | bytes accessed | tf_op | source)
XLA Modules:
  0.0 32.8 jit_solution(622686401498651362)
XLA Ops:
  0.7 31.5 %shard_map.82 = bf16[4,4,32,32]{3,2,1,0:T(8,128)(2,1)S(1)} custom-call(bf16[128,32]{1,0:T(8,128)(2,1)} %bitcast.12, bf16[128,128]{1,0:T(8,128)(2,1)} %bitcast.13, bf16[27,3,16]{2,1,0:T(4,128)(2,1)} %bitcast.14, f32[1,16]{1,0:T(1,128)} %bitcast.16, bf16[81,16,16]{2,1,0:T(8,128)(2,1)} %bitcast.11, f32[1,16]{1,0:T(1,128)} %bitcast.17, ...), custom_call_target="tpu_custom_call" | custom-call | tf_op jit(solution)/shard_map/pallas_call | solution.py:460
  32.1 0.7 %copy.10 = bf16[1,4,4,32,32]{4,3,2,1,0:T(8,128)(2,1)} copy(bf16[1,4,4,32,32]{4,3,2,1,0:T(8,128)(2,1)S(1)} %bitcast.10) | data formatting | bytes 65536

commit v4 on v3

--- a/solution.py
+++ b/solution.py
@@ -101,7 +101,7 @@
 
 def volume_kernel(ns, nt, meanwhile, src_hbm, tgt_hbm, c1_hbm, b1_hbm, c2_hbm, b2_hbm, c3_hbm, b3_ref,
                   vol, w1, w2, w3, bias,
-                  src, gs, gt, own, c1, c2, c3, bs, flat1, flat3, load,
+                  src, gs, gt, normed, own, c1, c2, c3, bs, flat1, flat3, load,
                   z_send, z_recv, y_send, y_recv, c_send, c_recv, x_send, x_recv, p_send, p_recv,
                   f_send, f_recv, h_send, h_recv):
     s, t = lax.axis_index("src"), lax.axis_index("tgt")
@@ -208,7 +208,7 @@
     p_go(1).start()
     y_go(0).start()
     c_go(0, 1).start()
-    for r in range(1, nx):
+    for r in far:
         x_go(r).start()
     c_go(0, 0).start()
 
@@ -240,17 +240,6 @@
             bias[1] = column(bs[1])
             bias[2] = jnp.full((16, 128), b3_ref[0, 0], F32)
 
-    for r in range(1, nx):
-        x_come(r).wait_recv()
-    for r in range(1, nx):
-        for m in range(2):
-            f_come(r, m).wait_recv()
-    sq = None
-    for n in range(ns):
-        v = gt[n].astype(F32)
-        sq = v * v if sq is None else sq + v * v
-    inv_t = inverse_root(jnp.sum(sq, axis=1, keepdims=True) + EPS)
-
     for q in range(nz):
         y_come(q).wait_recv()
         for w in range(2):
@@ -263,14 +252,26 @@
             p = v[8 * q:8 * q + 8]
             sq = p if sq is None else sq + p
     inv_s = inverse_root(jnp.sum(sq, axis=0, keepdims=True) + EPS)
-
     per = ch_t // ch_s
+    for n in range(ns):
+        left = jnp.concatenate([gs[n * per + q] for q in range(per)], 0)
+        normed[n] = (left.astype(F32) * inv_s).astype(BF)
+
+    for r in range(1, nx):
+        x_come(r).wait_recv()
+    for r in range(1, nx):
+        for m in range(2):
+            f_come(r, m).wait_recv()
+    sq = None
+    for n in range(ns):
+        v = gt[n].astype(F32)
+        sq = v * v if sq is None else sq + v * v
+    inv_t = inverse_root(jnp.sum(sq, axis=1, keepdims=True) + EPS)
+
     acc = jnp.zeros((128, 128), F32)
     for n in range(ns):
-        left = jnp.concatenate([gs[n * per + q] for q in range(per)], 0)
-        left = (left.astype(F32) * inv_s).astype(BF)
         right = (gt[n].astype(F32) * inv_t).astype(BF)
-        acc = acc + jnp.dot(right, left, preferred_element_type=F32)
+        acc = acc + jnp.dot(right, normed[n], preferred_element_type=F32)
     v = acc.T
     block = iota((8, 128), 1) // 32
     for i in range(4):
@@ -369,8 +370,7 @@
     def layer_one(lo, hi):
         b1 = bias_ref[0]
 
-        @pl.loop(lo, hi)
-        def _(i):
+        for i in range(lo, hi):
             for kk in range(2):
                 for q in range(3):
                     cols = []
@@ -390,8 +390,7 @@
 
     def rest():
         b2 = bias_ref[1]
-        @pl.loop(0, 3)
-        def _(ii):
+        for ii in range(3):
             for kk in range(3):
                 for p in range(4):
                     cols = []
@@ -468,6 +467,7 @@
             vmem((10, 10, 48, 128), BF), vmem((8, 8, 10, 16, 128), BF), vmem((6, 6, 10, 16, 128), BF),
             vmem((4, 64, 128), F32),
             vmem(src.shape, BF), vmem((nt, src.shape[-1], 128), BF), vmem((ns, 128, tgt.shape[-1]), BF),
+            vmem((ns, 128, tgt.shape[-1]), BF),
             vmem((4, 4, 8, 128), BF),
             vmem((27, 3, 16), BF), vmem((81, 16, 16), BF), vmem((27, 3, 16), BF), vmem((2, 1, 16), F32),
             vmem((128, 128), F32), vmem((128, 128), F32),

time: 32.9 us -> 30.3 us (0.921)
  Pallas kernels: 31.5 us -> 28.9 us
    pallas_call x1, Pallas kernels: 31.5 us -> 28.9 us  [whole_call(): pl.pallas_call(functools.partial(whole_kernel, ns, nt), out_shape=pltpu.V...]
where the time goes in v4:
time: 30.3 us; the launch traced here: 30.2 us
  Pallas kernels  28.9 us (95%)
  local copies, waits for them, and re-layouts  0.66 us (2%)
  between operations  0.66 us (2%)
    pallas_call x1, Pallas kernels, whole_call(): pl.pallas_call(functools.partial(whole_kernel, ns, nt), out_shape=pltpu.V...  28.9 us
    unnamed x1, local copies, waits for them, and re-layouts  0.66 us

profile of v4, /device:TPU:1, one launch (start us, length us, event | category | flops | bytes accessed | tf_op | source)
XLA Modules:
  0.0 30.2 jit_solution(3421425335604572123)
XLA Ops:
  0.7 28.9 %shard_map.82 = bf16[4,4,32,32]{3,2,1,0:T(8,128)(2,1)S(1)} custom-call(bf16[128,32]{1,0:T(8,128)(2,1)} %bitcast.12, bf16[128,128]{1,0:T(8,128)(2,1)} %bitcast.13, bf16[27,3,16]{2,1,0:T(4,128)(2,1)} %bitcast.14, f32[1,16]{1,0:T(1,128)} %bitcast.16, bf16[81,16,16]{2,1,0:T(8,128)(2,1)} %bitcast.11, f32[1,16]{1,0:T(1,128)} %bitcast.17, ...), custom_call_target="tpu_custom_call" | custom-call | tf_op jit(solution)/shard_map/pallas_call | solution.py:459
  29.6 0.7 %copy.10 = bf16[1,4,4,32,32]{4,3,2,1,0:T(8,128)(2,1)} copy(bf16[1,4,4,32,32]{4,3,2,1,0:T(8,128)(2,1)S(1)} %bitcast.10) | data formatting | bytes 65536

commit v5 on v4

--- a/solution.py
+++ b/solution.py
@@ -341,8 +341,7 @@
     dot = functools.partial(jnp.dot, preferred_element_type=F32)
 
     def pieces(lo, hi):
-        @pl.loop(lo, hi)
-        def _(i):
+        for i in range(lo, hi):
             for k in range(10):
                 u = u_ref[i, k].astype(F32)
                 before = jnp.where(lane >= 32, rolled(u, 32), 0.0)

time: 30.3 us -> 29.6 us (0.977)
  Pallas kernels: 28.9 us -> 28.2 us
    pallas_call x1, Pallas kernels: 28.9 us -> 28.2 us  [whole_call(): pl.pallas_call(functools.partial(whole_kernel, ns, nt), out_shape=pltpu.V...]
where the time goes in v5:
time: 29.6 us; the launch traced here: 29.5 us
  Pallas kernels  28.2 us (95%)
  local copies, waits for them, and re-layouts  0.66 us (2%)
  between operations  0.66 us (2%)
    pallas_call x1, Pallas kernels, whole_call(): pl.pallas_call(functools.partial(whole_kernel, ns, nt), out_shape=pltpu.V...  28.2 us
    unnamed x1, local copies, waits for them, and re-layouts  0.66 us

profile of v5, /device:TPU:1, one launch (start us, length us, event | category | flops | bytes accessed | tf_op | source)
XLA Modules:
  0.0 29.5 jit_solution(9152476290607948773)
XLA Ops:
  0.7 28.2 %shard_map.82 = bf16[4,4,32,32]{3,2,1,0:T(8,128)(2,1)S(1)} custom-call(bf16[128,32]{1,0:T(8,128)(2,1)} %bitcast.12, bf16[128,128]{1,0:T(8,128)(2,1)} %bitcast.13, bf16[27,3,16]{2,1,0:T(4,128)(2,1)} %bitcast.14, f32[1,16]{1,0:T(1,128)} %bitcast.16, bf16[81,16,16]{2,1,0:T(8,128)(2,1)} %bitcast.11, f32[1,16]{1,0:T(1,128)} %bitcast.17, ...), custom_call_target="tpu_custom_call" | custom-call | tf_op jit(solution)/shard_map/pallas_call | solution.py:458
  28.8 0.7 %copy.10 = bf16[1,4,4,32,32]{4,3,2,1,0:T(8,128)(2,1)} copy(bf16[1,4,4,32,32]{4,3,2,1,0:T(8,128)(2,1)S(1)} %bitcast.10) | data formatting | bytes 65536
